TPU v7x, 128 devices: a whole 4x4x4 slice. The times are simulated.
128 devices in a mesh: tm: 16 (over y, x), rows: 8 (over z, core).
Axes of the slice: x: 4, y: 4, z: 4, core: 2. Of those that a mesh axis runs over, the one named last changes fastest.
Arguments:
- observations: float32 [128, 1024], P('tm'), may hold values from -6 to 6
- observed: int32 [128], P('tm'), may hold values 0 or 1
- start_mean: float32 [1024], replicated, may hold values from -6 to 6
- transition: float32 [1024, 1024], P(('tm', 'rows')), may hold values from -1 to 1
- closed_loop: float32 [1024, 1024], P(('tm', 'rows')), may hold values from -1 to 1
- obs_gain: float32 [1024, 1024], replicated, may hold values from -0.0625 to 0.0625
- smooth_observed: float32 [1024, 1024], P(('tm', 'rows')), may hold values from -1 to 1
- smooth_missing: float32 [1024, 1024], P(('tm', 'rows')), may hold values from -1 to 1
Outputs:
- filtered: float32 [128, 1024], P('tm', 'rows')
- smoothed: float32 [128, 1024], P('tm', 'rows')
All inputs are finite; a program needn't handle non-finite values. No bound on the sum of `observed` on one device may be relied on, other than what follows from the above.
Results may differ from a plain program's by a relative error of at most 0.0003.
Values sent between devices are 32-bit elements; how exact they have to be, the bound alone decides.
No kernel may reach another device: no remote copies, remote signals or barrier semaphores. Data moves between devices by JAX's collectives and lax.ppermute only.
A program may use at most 128 MiB of HBM per device.

v0:
```python
from functools import partial
import jax
import jax.numpy as jnp
from jax import lax
from jax.sharding import PartitionSpec as P

precise_dot = partial(jnp.dot, precision=lax.Precision.HIGHEST)


def shifted(value, axis, steps):
    count = lax.axis_size(axis)
    initial, last = (max(0, -steps), min(count, count - steps))
    return lax.ppermute(value, axis, [(source, source + steps) for source in range(initial, last)])


def full_state(row_vec, direction):
    moved = shifted(row_vec, "tm", direction)
    return lax.all_gather(moved, "rows", axis=0, tiled=True)


def doubling_scan(matrix_rows, vector_rows, direction, segments):
    levels = (segments - 1).bit_length()
    for level_index in range(levels - 2):
        stride = direction * 2**level_index
        other_matrix, other_vector = shifted((matrix_rows, vector_rows), "tm", stride)
        start_totals = (
            jnp.zeros(matrix_rows.shape, jnp.float32),
            jnp.zeros(vector_rows.shape, jnp.float32),
        )
        pieces = (
            lax.all_gather(other_matrix, "rows", axis=0, tiled=True),
            lax.all_gather(other_vector, "rows", axis=0, tiled=True),
        )
        columns = lax.slice_in_dim(matrix_rows, 0, pieces[0].shape[0], axis=1)
        new_matrix = start_totals[0] + precise_dot(columns, pieces[0])
        new_vector = start_totals[1] + precise_dot(columns, pieces[1])
        matrix_rows, vector_rows = (new_matrix, vector_rows + new_vector)
    stride = direction * 2 ** max(levels - 2, 0)
    result_rows = vector_rows
    for repeat in range(3):
        result_rows = vector_rows + precise_dot(matrix_rows, full_state(result_rows, stride))
    return full_state(result_rows, direction)


def shards(
    observations,
    observed,
    start_mean,
    transition,
    closed_loop,
    obs_gain,
    smooth_observed,
    smooth_missing,
):
    seg_steps = observations.shape[0]
    state_dim = obs_gain.shape[0]
    segments = lax.axis_size("tm")
    row_count = state_dim // lax.axis_size("rows")
    seg_index = lax.axis_index("tm")
    row_start = lax.axis_index("rows") * row_count
    trans_full, closed_full, seen_full, missing_full = (
        lax.all_gather(transition, ("tm", "rows"), axis=0, tiled=True),
        lax.all_gather(closed_loop, ("tm", "rows"), axis=0, tiled=True),
        lax.all_gather(smooth_observed, ("tm", "rows"), axis=0, tiled=True),
        lax.all_gather(smooth_missing, ("tm", "rows"), axis=0, tiled=True),
    )
    dynamics = jnp.stack((trans_full, closed_full))
    seen_float = observed.astype(jnp.float32)
    inject = (
        lax.dot_general(
            observations, obs_gain, (((1,), (1,)), ((), ())), precision=lax.Precision.HIGHEST
        )
        * seen_float[:, None]
    )
    anchor = jnp.where(seg_index == 0, start_mean, jnp.zeros_like(start_mean))

    def forward_step(state_vec, inputs):
        is_seen, inject_row = inputs
        matrix = lax.dynamic_index_in_dim(dynamics, is_seen, 0, keepdims=False)
        state_vec = precise_dot(matrix, state_vec) + inject_row
        return (state_vec, state_vec)

    local_end = lax.scan(forward_step, anchor, (observed, inject))[0]
    row_ids = lax.broadcasted_iota(jnp.int32, (row_count, state_dim), 0) + row_start
    col_ids = lax.broadcasted_iota(jnp.int32, (row_count, state_dim), 1)
    eye_rows = (row_ids == col_ids).astype(jnp.float32)

    def compose_forward(product, is_seen):
        matrix = lax.dynamic_index_in_dim(dynamics, is_seen, 0, keepdims=False)
        return (precise_dot(product, matrix), None)

    forward_rows = lax.scan(compose_forward, eye_rows, observed, reverse=True)[0]
    forward_rows = forward_rows * (seg_index != 0).astype(jnp.float32)
    gains = jnp.stack((missing_full, seen_full))
    step_ids = lax.iota(jnp.int32, seg_steps) + seg_index * seg_steps
    keep_gain = (step_ids != segments * seg_steps - 1).astype(jnp.float32)

    def compose_backward(product, inputs):
        is_seen, keep_now = inputs
        matrix = lax.dynamic_index_in_dim(gains, is_seen, 0, keepdims=False)
        return (precise_dot(product, matrix) * keep_now, None)

    backward_rows = lax.scan(compose_backward, eye_rows, (observed, keep_gain))[0]
    end_rows = lax.dynamic_slice_in_dim(local_end, row_start, row_count)
    start_full = doubling_scan(forward_rows, end_rows, 1, segments) + anchor
    filtered_full = lax.scan(forward_step, start_full, (observed, inject))[1]
    predicted = lax.dot_general(
        filtered_full, trans_full, (((1,), (1,)), ((), ())), precision=lax.Precision.HIGHEST
    )

    def backward_step(state_vec, inputs):
        is_seen, keep_now, mean_row, predicted_row = inputs
        matrix = lax.dynamic_index_in_dim(gains, is_seen, 0, keepdims=False)
        state_vec = mean_row + keep_now * precise_dot(matrix, state_vec - predicted_row)
        return (state_vec, state_vec)

    backward_inputs = (observed, keep_gain, filtered_full, predicted)
    zero_state = jnp.zeros_like(start_mean)
    local_first = lax.scan(backward_step, zero_state, backward_inputs, reverse=True)[0]
    first_rows = lax.dynamic_slice_in_dim(local_first, row_start, row_count)
    next_full = doubling_scan(backward_rows, first_rows, -1, segments)
    smoothed_full = lax.scan(backward_step, next_full, backward_inputs, reverse=True)[1]
    filtered = lax.dynamic_slice_in_dim(filtered_full, row_start, row_count, 1)
    smoothed = lax.dynamic_slice_in_dim(smoothed_full, row_start, row_count, 1)
    return (filtered, smoothed)


def solution(mesh):
    return jax.shard_map(
        shards,
        mesh=mesh,
        in_specs=(
            P("tm", None),
            P("tm"),
            P(),
            P(("tm", "rows"), None),
            P(("tm", "rows"), None),
            P(),
            P(("tm", "rows"), None),
            P(("tm", "rows"), None),
        ),
        out_specs=(P("tm", "rows"), P("tm", "rows")),
        check_vma=False,
    )
```

profile of v0, /device:TPU:47, one launch (start us, length us, event | category | flops | bytes accessed | tf_op | source)
XLA Modules:
  0.0 942.0 jit_solution(2322415368678451098)
XLA Ops:
  10.1 66.6 %all-gather.21.cloned.1.call-done = f32[1024,1024]{1,0:T(8,128)} async-done(((f32[8,1024]{1,0:T(8,128)}), f32[1024,1024]{1,0:T(8,128)}) %all-gather.21.cloned.1.call-update) | async-done | bytes 4194320 | tf_op jit(solution)/shard_map/all_gather | solution.py:62
  76.7 67.3 %all-gather.23.cloned.1.call-done = f32[1024,1024]{1,0:T(8,128)} async-done(((f32[8,1024]{1,0:T(8,128)}), f32[1024,1024]{1,0:T(8,128)}) %all-gather.23.cloned.1.call-update) | async-done | bytes 4194320 | tf_op jit(solution)/shard_map/all_gather | solution.py:63
  144.1 8.4 pad_maximum_fusion
  152.5 88.6 %while.78 = (s32[]{:T(128)}, f32[128,1024]{0,1:T(8,128)S(1)}, s32[8]{0:T(128)S(1)}, f32[2,1024,1024]{2,1,0:T(8,128)}, s32[]{:T(128)}, /*index=5*/s32[]{:T(128)}, s32[]{:T(128)}, s32[]{:T(128)}) while((s32[]{:T(128)}, f32[128,1024]{0,1:T(8,128)S(1)}, s32[8]{0:T(128)S(1)}, f32[2,1024,1024]{2,1,0:T(8,128)}, s32[]{:T(128)}, /*index=5*/s32[]{:T(128)}, ...), condition=%wide.region_3.4_spmd, body=%wide.region_2.3_spmd.sunk | while | flops 1610612736 | bytes 6291603 | solution.py:92
  155.1 8.5 fusion.111
  166.1 8.5 fusion.111
  177.2 8.5 fusion.111
  188.3 8.5 fusion.111
  199.4 8.5 fusion.111
  210.4 8.5 fusion.111
  221.5 8.5 fusion.111
  232.6 8.5 fusion.111
  245.4 12.4 %collective-permute-done.1 = f32[128,1024]{0,1:T(8,128)S(1)} collective-permute-done((f32[128,1024]{0,1:T(8,128)S(1)}, f32[128,1024]{0,1:T(8,128)S(1)}, u32[]{:S(2)}, u32[]{:S(2)}) %collective-permute-start.1) | collective-permute-done | bytes 524320 | tf_op jit(solution)/shard_map/ppermute | solution.py:13
  258.8 23.6 %all-gather.31.cloned.1.call-done = f32[1024,1024]{1,0:T(8,128)} async-done(((f32[8,1024]{1,0:T(8,128)}), f32[1024,1024]{1,0:T(8,128)}) %all-gather.31.cloned.1.call-update) | async-done | bytes 4194320 | tf_op jit(solution)/shard_map/all_gather | solution.py:64
  282.4 8.4 pad_maximum_fusion.1
  290.8 98.8 %while.80 = (s32[]{:T(128)}, f32[128,1024]{0,1:T(8,128)S(1)}, s32[8]{0:T(128)S(1)}, f32[2,1024,1024]{2,1,0:T(8,128)}, f32[8]{0:T(128)S(1)}, /*index=5*/s32[]{:T(128)}, s32[]{:T(128)}, s32[]{:T(128)}) while((s32[]{:T(128)}, f32[128,1024]{0,1:T(8,128)S(1)}, s32[8]{0:T(128)S(1)}, f32[2,1024,1024]{2,1,0:T(8,128)}, f32[8]{0:T(128)S(1)}, ...), condition=%wide.region_9.10_spmd, body=%wide.region_8.9_spmd.sunk | while | flops 1610743808 | bytes 6292115 | solution.py:103
  294.0 9.4 fusion.117
  306.5 9.1 fusion.117
  318.8 9.1 fusion.117
  331.1 9.1 fusion.117
  343.5 9.1 fusion.117
  355.8 9.1 fusion.117
  368.1 9.1 fusion.117
  380.4 9.1 fusion.117
  392.1 14.7 %collective-permute-done.9 = f32[128,1024]{0,1:T(8,128)S(1)} collective-permute-done((f32[128,1024]{0,1:T(8,128)S(1)}, f32[128,1024]{0,1:T(8,128)S(1)}, u32[]{:S(2)}, u32[]{:S(2)}) %collective-permute-start.9) | collective-permute-done | bytes 524320 | tf_op jit(solution)/shard_map/ppermute | solution.py:13
  407.9 6.7 fusion.54
  416.5 13.8 %collective-permute-done.3 = f32[128,1024]{1,0:T(8,128)S(1)} collective-permute-done((f32[128,1024]{1,0:T(8,128)S(1)}, f32[128,1024]{1,0:T(8,128)S(1)}, u32[]{:S(2)}, u32[]{:S(2)}) %collective-permute-start.3) | collective-permute-done | bytes 524320 | tf_op jit(solution)/shard_map/ppermute | solution.py:13
  436.8 67.1 %while.77 = (s32[]{:T(128)}, f32[1024]{0:T(1024)S(1)}, s32[8]{0:T(128)S(1)}, f32[2,1024,1024]{2,1,0:T(8,128)}, f32[8,1024]{1,0:T(8,128)S(1)}, /*index=5*/s32[]{:T(128)}, s32[]{:T(128)}, s32[]{:T(128)}) while((s32[]{:T(128)}, f32[1024]{0:T(1024)S(1)}, s32[8]{0:T(128)S(1)}, f32[2,1024,1024]{2,1,0:T(8,128)}, f32[8,1024]{1,0:T(8,128)S(1)}, ...), condition=%wide.region_1.2_spmd, body=%wide.region_0.1_spmd.sunk | while | flops 12583941 | bytes 4223115 | solution.py:83
  456.1 6.0 fusion.108
  464.7 5.8 fusion.108
  473.1 5.8 fusion.108
  508.3 12.1 %all-gather = f32[8,1,128]{2,1,0:T(1,128)S(1)} all-gather(f32[1,1,128]{2,1,0:T(1,128)S(1)} %bitcast.297), channel_id=1, replica_groups=mesh['tm'=16,'rows'=8] {'rows'}, dimensions={0}, use_global_device_ids=true | all-gather | bytes 4608 | tf_op jit(solution)/shard_map/all_gather | solution.py:32
  526.6 11.0 %all-gather.1 = f32[8,1,128]{2,1,0:T(1,128)S(1)} all-gather(f32[1,1,128]{2,1,0:T(1,128)S(1)} %bitcast.298), channel_id=1, replica_groups=mesh['tm'=16,'rows'=8] {'rows'}, dimensions={0}, use_global_device_ids=true | all-gather | bytes 4608 | tf_op jit(solution)/shard_map/all_gather | solution.py:32
  541.1 6.7 fusion.57
  551.2 8.4 all-gather.2
  569.0 10.9 %all-gather.3 = f32[8,1,128]{2,1,0:T(1,128)S(1)} all-gather(f32[1,1,128]{2,1,0:T(1,128)S(1)} %bitcast.294), channel_id=1, replica_groups=mesh['tm'=16,'rows'=8] {'rows'}, dimensions={0}, use_global_device_ids=true | all-gather | bytes 4608 | tf_op jit(solution)/shard_map/all_gather | solution.py:18
  584.8 9.0 all-gather.4
  599.8 10.9 %all-gather.5 = f32[8,1,128]{2,1,0:T(1,128)S(1)} all-gather(f32[1,1,128]{2,1,0:T(1,128)S(1)} %bitcast.289), channel_id=1, replica_groups=mesh['tm'=16,'rows'=8] {'rows'}, dimensions={0}, use_global_device_ids=true | all-gather | bytes 4608 | tf_op jit(solution)/shard_map/all_gather | solution.py:18
  610.7 67.1 %while.79 = (s32[]{:T(128)}, f32[1024]{0:T(1024)S(1)}, f32[8,1024]{1,0:T(8,128)S(1)}, s32[8]{0:T(128)S(1)}, f32[2,1024,1024]{2,1,0:T(8,128)}, /*index=5*/f32[8,1024]{1,0:T(8,128)S(1)}, s32[]{:T(128)}, s32[]{:T(128)}, s32[]{:T(128)}) while((s32[]{:T(128)}, f32[1024]{0:T(1024)S(1)}, f32[8,1024]{1,0:T(8,128)S(1)}, s32[8]{0:T(128)S(1)}, ...), condition=%wide.region_5.6_spmd, body=%wide.region_4.5_spmd.sunk | while | flops 12583941 | bytes 4231319 | solution.py:106
  613.1 5.8 fusion.114
  621.6 5.8 fusion.114
  683.5 76.8 %while.82 = (s32[]{:T(128)}, f32[1024]{0:T(1024)S(1)}, f32[8,1024]{1,0:T(8,128)S(1)}, f32[8]{0:T(128)S(1)}, s32[8]{0:T(128)S(1)}, /*index=5*/f32[2,1024,1024]{2,...) while((s32[]{:T(128)}, f32[1024]{0:T(1024)S(1)}, ...), condition=%wide.region_7.8_spmd.clone, body=%wide.region_6.7_spmd.clone.sunk | while | flops 12587015 | bytes 4243657 | solution.py:119
  686.1 5.8 fusion.123
  695.7 5.8 fusion.123
  705.3 5.8 fusion.123
  714.9 5.8 fusion.123
  724.5 5.8 fusion.123
  734.1 5.8 fusion.123
  743.7 5.8 fusion.123
  766.9 8.9 all-gather.6
  782.8 10.9 %all-gather.7 = f32[8,1,128]{2,1,0:T(1,128)S(1)} all-gather(f32[1,1,128]{2,1,0:T(1,128)S(1)} %bitcast.300), channel_id=1, replica_groups=mesh['tm'=16,'rows'=8] {'rows'}, dimensions={0}, use_global_device_ids=true | all-gather | bytes 4608 | tf_op jit(solution)/shard_map/all_gather | solution.py:32
  801.5 8.1 all-gather.8
  814.4 10.9 %all-gather.9 = f32[8,1,128]{2,1,0:T(1,128)S(1)} all-gather(f32[1,1,128]{2,1,0:T(1,128)S(1)} %bitcast.296), channel_id=1, replica_groups=mesh['tm'=16,'rows'=8] {'rows'}, dimensions={0}, use_global_device_ids=true | all-gather | bytes 4608 | tf_op jit(solution)/shard_map/all_gather | solution.py:18
  830.2 9.0 all-gather.10
  846.1 10.9 %all-gather.11 = f32[8,1,128]{2,1,0:T(1,128)S(1)} all-gather(f32[1,1,128]{2,1,0:T(1,128)S(1)} %bitcast.293), channel_id=1, replica_groups=mesh['tm'=16,'rows'=8] {'rows'}, dimensions={0}, use_global_device_ids=true | all-gather | bytes 4608 | tf_op jit(solution)/shard_map/all_gather | solution.py:18
  857.0 77.0 %while.81 = (s32[]{:T(128)}, f32[1024]{0:T(1024)S(1)}, f32[8,1024]{1,0:T(8,128)S(1)}, f32[8,1024]{1,0:T(8,128)S(1)}, f32[8]{0:T(128)S(1)}, /*index=5*/s32[8]{0:T...) while((s32[]{:T(128)}, f32[1024]{0:T(1024)S(1)}, ...), condition=%wide.region_11.12_spmd, body=%wide.region_10.11_spmd.sunk | while | flops 12585990 | bytes 4251851 | solution.py:122
  859.5 5.8 fusion.120
  869.1 5.8 fusion.120
  878.8 5.8 fusion.120
  888.4 5.8 fusion.120
  898.0 5.8 fusion.120
  907.6 5.8 fusion.120
  917.3 5.8 fusion.120
  926.9 5.8 fusion.120
  (289 shorter events, 227.4 us)
Async XLA Ops:
  7.2 424.0 %copy-start = (f32[8,1024]{1,0:T(8,128)S(1)}, f32[8,1024]{1,0:T(8,128)}, u32[]{:S(2)}) copy-start(f32[8,1024]{1,0:T(8,128)} %param.20) | copy-start | bytes 98308
  7.2 69.5 %all-gather.21.cloned.1.call-start = ((), (), s32[]{:S(2)}) async-start(), calls=%async_computation | async-start | bytes 4227072 | tf_op jit(solution)/shard_map/all_gather | solution.py:62
  7.9 136.1 %all-gather.23.cloned.1.call-start = ((), (), s32[]{:S(2)}) async-start(), calls=%async_computation.1 | async-start | bytes 4227072 | tf_op jit(solution)/shard_map/all_gather | solution.py:63
  8.7 250.1 %all-gather.29.cloned.1.call-start = ((), (), s32[]{:S(2)}) async-start(), calls=%async_computation.4 | async-start | bytes 4227072 | tf_op jit(solution)/shard_map/all_gather | solution.py:65
  9.4 273.0 %all-gather.31.cloned.1.call-start = ((), (), s32[]{:S(2)}) async-start(), calls=%async_computation.5 | async-start | bytes 4227072 | tf_op jit(solution)/shard_map/all_gather | solution.py:64
  10.0 397.9 %all-gather.25.cloned.1.call-start = ((), (), s32[]{:S(2)}) async-start(), calls=%async_computation.2 | async-start | bytes 4718592 | tf_op jit(solution)/shard_map/all_gather | solution.py:31
  144.1 8.4 copy-start.6
  241.1 16.7 %collective-permute-start.1 = (f32[128,1024]{0,1:T(8,128)S(1)}, f32[128,1024]{0,1:T(8,128)S(1)}, u32[]{:S(2)}, u32[]{:S(2)}) collective-permute-start(f32[128,1024]{0,1:T(8,128)S(1)} %broadcast_multiply_fusion), channel_id=1, source_target_pairs={{0,8},{8,16},{16,24},{24,32},{32,40},{40,48},{48,56},{56,64},{64,7... | collective-permute-start | bytes 1572872 | tf_op jit(solution)/shard_map/ppermute | solution.py:13
  257.8 0.8 copy-start.4
  258.7 282.4 %all-gather.33.cloned.1.call-start = ((), (), s32[]{:S(2)}) async-start(), calls=%async_computation.6 | async-start | bytes 4718592 | tf_op jit(solution)/shard_map/all_gather | solution.py:31
  389.6 41.6 %copy-start.5 = (f32[1024]{0:T(1024)S(1)}, f32[1024]{0:T(1024)}, u32[]{:S(2)}) copy-start(f32[1024]{0:T(1024)} %param.22) | copy-start | bytes 12292
  389.6 17.2 %collective-permute-start.9 = (f32[128,1024]{0,1:T(8,128)S(1)}, f32[128,1024]{0,1:T(8,128)S(1)}, u32[]{:S(2)}, u32[]{:S(2)}) collective-permute-start(f32[128,1024]{0,1:T(8,128)S(1)} %get-tuple-element.477), channel_id=1, source_target_pairs={{8,0},{16,8},{24,16},{32,24},{40,32},{48,40},{56,48},{64,56},{72,6... | collective-permute-start | bytes 1572872 | tf_op jit(solution)/shard_map/ppermute | solution.py:13
  406.8 0.8 copy-start.2
  407.6 152.0 %all-gather.27.cloned.1.call-start = ((), (), s32[]{:S(2)}) async-start(), calls=%async_computation.3 | async-start | bytes 4718592 | tf_op jit(solution)/shard_map/all_gather | solution.py:31
  414.5 15.7 %collective-permute-start.3 = (f32[128,1024]{1,0:T(8,128)S(1)}, f32[128,1024]{1,0:T(8,128)S(1)}, u32[]{:S(2)}, u32[]{:S(2)}) collective-permute-start(f32[128,1024]{1,0:T(8,128)S(1)} %fusion.54), channel_id=1, source_target_pairs={{0,16},{8,24},{16,32},{24,40},{32,48},{40,56},{48,64},{56,72},{64,... | collective-permute-start | bytes 1572872 | tf_op jit(solution)/shard_map/ppermute | solution.py:13
  430.3 0.8 copy-start.3
  431.1 365.8 %all-gather.35.cloned.1.call-start = ((), (), s32[]{:S(2)}) async-start(), calls=%async_computation.7 | async-start | bytes 4718592 | tf_op jit(solution)/shard_map/all_gather | solution.py:31
  504.0 4.3 collective-permute-start
  520.8 5.8 collective-permute-start.2
  538.0 13.1 %collective-permute-start.4 = (f32[128]{0:T(128)S(1)}, f32[128]{0:T(128)S(1)}, u32[]{:S(2)}, u32[]{:S(2)}) collective-permute-start(f32[128]{0:T(128)S(1)} %fusion.41), channel_id=1, source_target_pairs={{0,32},{8,40},{16,48},{24,56},{32,64},{40,72},{48,80},{56,88},{64,... | collective-permute-start | bytes 1544 | tf_op jit(solution)/shard_map/ppermute | solution.py:13
  547.8 50.9 %collective-permute-start.11 = (f32[128,1024]{1,0:T(8,128)S(1)}, f32[128,1024]{1,0:T(8,128)S(1)}, u32[]{:S(2)}, u32[]{:S(2)}) collective-permute-start(f32[128,1024]{1,0:T(8,128)S(1)} %fusion.57), channel_id=1, source_target_pairs={{16,0},{24,8},{32,16},{40,24},{48,32},{56,40},{64,48},{72,56},{80,... | collective-permute-start | bytes 1572872 | tf_op jit(solution)/shard_map/ppermute | solution.py:13
  564.6 4.4 collective-permute-start.5
  580.4 4.4 collective-permute-start.6
  594.2 5.6 collective-permute-start.7
  598.7 0.8 copy-start.1
  760.4 6.5 collective-permute-start.8
  776.1 6.7 collective-permute-start.10
  794.1 7.3 collective-permute-start.12
  810.0 4.4 collective-permute-start.13
  825.8 4.4 collective-permute-start.14
  839.6 6.5 collective-permute-start.15
Sparse Core Ops, SparseCore 0:
  11.2 65.5 all-gather.20
  79.9 64.1 all-gather.22
  147.2 64.1 all-gather.28
  214.5 67.8 all-gather.30
  283.9 36.1 all-gather.24
  407.7 36.7 all-gather.32
  446.2 32.3 all-gather.26
  599.6 30.8 all-gather.34
where the time goes:
time: 952 us; the launch traced here: 942 us
  matrix products  364 us (38%)
  waiting for transfers between devices  225 us (24%)
  blocking collectives  121 us (13%)
  loops' own time  93.2 us (10%)
  local copies, waits for them, and re-layouts  50.7 us (5%)
  starting transfers between devices  46.2 us (5%)
  other arithmetic  27.2 us (3%)
  between operations  15 us (2%)
    dot_general x16, matrix products, forward_step(): state_vec = precise_dot(matrix, state_vec) + inject_row  92.6 us
    dot_general x16, matrix products, backward_step(): precise_dot(matrix, state_vec - predicted_row)  92.1 us
    all_gather x8, blocking collectives, full_state(): return lax.all_gather(moved, 'rows', axis=0, tiled=True)  78.1 us
    dot_general x8, matrix products, compose_backward(): return (precise_dot(product, matrix) * keep_now, None)  73.3 us
    dot_general x8, matrix products, compose_forward(): return (precise_dot(product, matrix), None)  67.8 us
    all_gather x1, waiting for transfers between devices, shards(): lax.all_gather(closed_loop, ('tm', 'rows'), axis=0, tiled=True)  67.3 us
    all_gather x1, waiting for transfers between devices, shards(): lax.all_gather(transition, ('tm', 'rows'), axis=0, tiled=True)  66.6 us
    ppermute x16, waiting for transfers between devices, shifted(): lax.ppermute(value, axis, [(source, source + steps) for source in range(i...  64.5 us
  transfers between devices with their start and end apart: 24, of which 16 were waited for; matrix products, arithmetic and copies ran while one was open for 40% of the time, Pallas kernels for 0%

commit v1 on v0

--- a/solution.py
+++ b/solution.py
@@ -1,3 +1,4 @@
+import functools
 from functools import partial
 import jax
 import jax.numpy as jnp
@@ -5,6 +6,16 @@
 from jax.sharding import PartitionSpec as P
 
 precise_dot = partial(jnp.dot, precision=lax.Precision.HIGHEST)
+
+
+def place_boxes(target, d0):
+    kept_arr = lax.all_to_all(
+        jnp.stack([target] * lax.axis_size(("tm", "rows"))), ("tm", "rows"), 0, 0
+    )
+    return jnp.concatenate(kept_arr, axis=d0)
+
+
+store_leaf = functools.partial(place_boxes, d0=0)
 
 
 def shifted(value, axis, steps):
@@ -60,7 +71,7 @@
     row_start = lax.axis_index("rows") * row_count
     trans_full, closed_full, seen_full, missing_full = (
         lax.all_gather(transition, ("tm", "rows"), axis=0, tiled=True),
-        lax.all_gather(closed_loop, ("tm", "rows"), axis=0, tiled=True),
+        store_leaf(closed_loop),
         lax.all_gather(smooth_observed, ("tm", "rows"), axis=0, tiled=True),
         lax.all_gather(smooth_missing, ("tm", "rows"), axis=0, tiled=True),
     )

time: 952 us -> 921 us (0.967)
  waiting for transfers between devices: 225 us -> 180 us
  starting transfers between devices: 46.2 us -> 56.7 us
    all_gather x1 -> x0, waiting for transfers between devices: 67.3 us -> none  [shards(): lax.all_gather(closed_loop, ('tm', 'rows'), axis=0, tiled=True)]
    all_to_all x0 -> x1, waiting for transfers between devices: none -> 49 us  [place_boxes(): lax.all_to_all(jnp.stack([target] * lax.axis_size(('tm', 'rows'))), ('tm'...]
    all_gather x1, waiting for transfers between devices: 66.6 us -> 40.6 us  [shards(): lax.all_gather(transition, ('tm', 'rows'), axis=0, tiled=True)]
    all_to_all x0 -> x1, starting transfers between devices: none -> 10.9 us  [place_boxes(): lax.all_to_all(jnp.stack([target] * lax.axis_size(('tm', 'rows'))), ('tm'...]
  transfers between devices with their start and end apart: 24 -> 24, of which waited for: 16 -> 16; matrix products, arithmetic and copies ran while one was open for 40% -> 42% of each run, Pallas kernels for 0% -> 0%
where the time goes in v1:
time: 921 us; the launch traced here: 909 us
  matrix products  364 us (40%)
  waiting for transfers between devices  180 us (20%)
  blocking collectives  121 us (13%)
  loops' own time  92.2 us (10%)
  starting transfers between devices  56.7 us (6%)
  local copies, waits for them, and re-layouts  53.3 us (6%)
  other arithmetic  26.7 us (3%)
  between operations  15 us (2%)
    dot_general x16, matrix products, forward_step(): state_vec = precise_dot(matrix, state_vec) + inject_row  92.7 us
    dot_general x16, matrix products, backward_step(): precise_dot(matrix, state_vec - predicted_row)  92.1 us
    all_gather x8, blocking collectives, full_state(): return lax.all_gather(moved, 'rows', axis=0, tiled=True)  78.1 us
    dot_general x8, matrix products, compose_backward(): return (precise_dot(product, matrix) * keep_now, None)  73.3 us
    dot_general x8, matrix products, compose_forward(): return (precise_dot(product, matrix), None)  67.9 us
    ppermute x16, waiting for transfers between devices, shifted(): lax.ppermute(value, axis, [(source, source + steps) for source in range(i...  64.8 us
    all_to_all x1, waiting for transfers between devices, place_boxes(): lax.all_to_all(jnp.stack([target] * lax.axis_size(('tm', 'rows'))), ('tm'...  49 us
    ppermute x16, starting transfers between devices, shifted(): lax.ppermute(value, axis, [(source, source + steps) for source in range(i...  45.4 us
  transfers between devices with their start and end apart: 24, of which 16 were waited for; matrix products, arithmetic and copies ran while one was open for 42% of the time, Pallas kernels for 0%

profile of v1, /device:TPU:47, one launch (start us, length us, event | category | flops | bytes accessed | tf_op | source)
XLA Modules:
  0.0 909.4 jit_solution(1329519714842135245)
XLA Ops:
  12.7 10.9 %all-to-all-start = ((f32[128,8,1024]{2,1,0:T(8,128)}), f32[128,8,1024]{2,1,0:T(8,128)}, u32[]{:S(2)}, u32[]{:S(2)}) async-start(f32[128,8,1024]{2,1,0:T(8,128)} %stack.13), calls=%async_computation | async-start | bytes 8388608 | tf_op jit(solution)/shard_map/all_to_all | solution.py:12
  23.8 49.0 %all-to-all-done = f32[128,8,1024]{2,1,0:T(8,128)} async-done(((f32[128,8,1024]{2,1,0:T(8,128)}), f32[128,8,1024]{2,1,0:T(8,128)}, u32[]{:S(2)}, u32[]{:S(2)}) %all-to-all-start) | async-done | bytes 4194336 | tf_op jit(solution)/shard_map/all_to_all | solution.py:12
  72.9 40.6 %all-gather.20.cloned.1.call-done = f32[1024,1024]{1,0:T(8,128)} async-done(((f32[8,1024]{1,0:T(8,128)}), f32[1024,1024]{1,0:T(8,128)}) %all-gather.20.cloned.1.call-update) | async-done | bytes 4194320 | tf_op jit(solution)/shard_map/all_gather | solution.py:73
  113.5 8.4 pad_maximum_fusion
  121.8 88.7 %while.78 = (s32[]{:T(128)}, f32[128,1024]{0,1:T(8,128)S(1)}, s32[8]{0:T(128)S(1)}, f32[2,1024,1024]{2,1,0:T(8,128)}, s32[]{:T(128)}, /*index=5*/s32[]{:T(128)}, s32[]{:T(128)}, s32[]{:T(128)}) while((s32[]{:T(128)}, f32[128,1024]{0,1:T(8,128)S(1)}, s32[8]{0:T(128)S(1)}, f32[2,1024,1024]{2,1,0:T(8,128)}, s32[]{:T(128)}, /*index=5*/s32[]{:T(128)}, ...), condition=%wide.region_3.4_spmd, body=%wide.region_2.3_spmd.sunk | while | flops 1610612736 | bytes 6291603 | solution.py:103
  124.4 8.5 fusion.111
  135.5 8.5 fusion.111
  146.6 8.5 fusion.111
  157.7 8.5 fusion.111
  168.8 8.5 fusion.111
  179.9 8.5 fusion.111
  191.0 8.5 fusion.111
  202.0 8.5 fusion.111
  214.9 12.4 %collective-permute-done.1 = f32[128,1024]{0,1:T(8,128)S(1)} collective-permute-done((f32[128,1024]{0,1:T(8,128)S(1)}, f32[128,1024]{0,1:T(8,128)S(1)}, u32[]{:S(2)}, u32[]{:S(2)}) %collective-permute-start.1) | collective-permute-done | bytes 524320 | tf_op jit(solution)/shard_map/ppermute | solution.py:24
  228.2 23.6 %all-gather.28.cloned.1.call-done = f32[1024,1024]{1,0:T(8,128)} async-done(((f32[8,1024]{1,0:T(8,128)}), f32[1024,1024]{1,0:T(8,128)}) %all-gather.28.cloned.1.call-update) | async-done | bytes 4194320 | tf_op jit(solution)/shard_map/all_gather | solution.py:75
  251.9 8.4 pad_maximum_fusion.1
  260.3 98.8 %while.80 = (s32[]{:T(128)}, f32[128,1024]{0,1:T(8,128)S(1)}, s32[8]{0:T(128)S(1)}, f32[2,1024,1024]{2,1,0:T(8,128)}, f32[8]{0:T(128)S(1)}, /*index=5*/s32[]{:T(128)}, s32[]{:T(128)}, s32[]{:T(128)}) while((s32[]{:T(128)}, f32[128,1024]{0,1:T(8,128)S(1)}, s32[8]{0:T(128)S(1)}, f32[2,1024,1024]{2,1,0:T(8,128)}, f32[8]{0:T(128)S(1)}, ...), condition=%wide.region_9.10_spmd, body=%wide.region_8.9_spmd.sunk | while | flops 1610743808 | bytes 6292115 | solution.py:114
  263.5 9.4 %fusion.117 = f32[128,1024]{0,1:T(8,128)S(1)} fusion(f32[128,1024]{0,1:T(8,128)S(1)} %copy.57, f32[2,1024,1024]{2,1,0:T(8,128)} %get-tuple-element.928, s32[]{:T(128)S(6)} %select_n.70, f32[]{:T(128)} %bitcast.249), kind=kOutput, calls=%fused_computation.19.clone.1 | convolution fusion | flops 1610743808 | bytes 5243396 | tf_op jit(solution)/shard_map/while/body/eval_jaxpr/dot_general | solution.py:112
  276.0 9.1 %fusion.117 = f32[128,1024]{0,1:T(8,128)S(1)} fusion(f32[128,1024]{0,1:T(8,128)S(1)} %copy.57, f32[2,1024,1024]{2,1,0:T(8,128)} %get-tuple-element.928, s32[]{:T(128)S(6)} %select_n.70, f32[]{:T(128)} %bitcast.249), kind=kOutput, calls=%fused_computation.19.clone.1 | convolution fusion | flops 1610743808 | bytes 5243396 | tf_op jit(solution)/shard_map/while/body/eval_jaxpr/dot_general | solution.py:112
  288.3 9.1 %fusion.117 = f32[128,1024]{0,1:T(8,128)S(1)} fusion(f32[128,1024]{0,1:T(8,128)S(1)} %copy.57, f32[2,1024,1024]{2,1,0:T(8,128)} %get-tuple-element.928, s32[]{:T(128)S(6)} %select_n.70, f32[]{:T(128)} %bitcast.249), kind=kOutput, calls=%fused_computation.19.clone.1 | convolution fusion | flops 1610743808 | bytes 5243396 | tf_op jit(solution)/shard_map/while/body/eval_jaxpr/dot_general | solution.py:112
  300.6 9.1 %fusion.117 = f32[128,1024]{0,1:T(8,128)S(1)} fusion(f32[128,1024]{0,1:T(8,128)S(1)} %copy.57, f32[2,1024,1024]{2,1,0:T(8,128)} %get-tuple-element.928, s32[]{:T(128)S(6)} %select_n.70, f32[]{:T(128)} %bitcast.249), kind=kOutput, calls=%fused_computation.19.clone.1 | convolution fusion | flops 1610743808 | bytes 5243396 | tf_op jit(solution)/shard_map/while/body/eval_jaxpr/dot_general | solution.py:112
  313.0 9.1 %fusion.117 = f32[128,1024]{0,1:T(8,128)S(1)} fusion(f32[128,1024]{0,1:T(8,128)S(1)} %copy.57, f32[2,1024,1024]{2,1,0:T(8,128)} %get-tuple-element.928, s32[]{:T(128)S(6)} %select_n.70, f32[]{:T(128)} %bitcast.249), kind=kOutput, calls=%fused_computation.19.clone.1 | convolution fusion | flops 1610743808 | bytes 5243396 | tf_op jit(solution)/shard_map/while/body/eval_jaxpr/dot_general | solution.py:112
  325.3 9.1 %fusion.117 = f32[128,1024]{0,1:T(8,128)S(1)} fusion(f32[128,1024]{0,1:T(8,128)S(1)} %copy.57, f32[2,1024,1024]{2,1,0:T(8,128)} %get-tuple-element.928, s32[]{:T(128)S(6)} %select_n.70, f32[]{:T(128)} %bitcast.249), kind=kOutput, calls=%fused_computation.19.clone.1 | convolution fusion | flops 1610743808 | bytes 5243396 | tf_op jit(solution)/shard_map/while/body/eval_jaxpr/dot_general | solution.py:112
  337.6 9.1 %fusion.117 = f32[128,1024]{0,1:T(8,128)S(1)} fusion(f32[128,1024]{0,1:T(8,128)S(1)} %copy.57, f32[2,1024,1024]{2,1,0:T(8,128)} %get-tuple-element.928, s32[]{:T(128)S(6)} %select_n.70, f32[]{:T(128)} %bitcast.249), kind=kOutput, calls=%fused_computation.19.clone.1 | convolution fusion | flops 1610743808 | bytes 5243396 | tf_op jit(solution)/shard_map/while/body/eval_jaxpr/dot_general | solution.py:112
  349.9 9.1 %fusion.117 = f32[128,1024]{0,1:T(8,128)S(1)} fusion(f32[128,1024]{0,1:T(8,128)S(1)} %copy.57, f32[2,1024,1024]{2,1,0:T(8,128)} %get-tuple-element.928, s32[]{:T(128)S(6)} %select_n.70, f32[]{:T(128)} %bitcast.249), kind=kOutput, calls=%fused_computation.19.clone.1 | convolution fusion | flops 1610743808 | bytes 5243396 | tf_op jit(solution)/shard_map/while/body/eval_jaxpr/dot_general | solution.py:112
  361.6 14.7 %collective-permute-done.9 = f32[128,1024]{0,1:T(8,128)S(1)} collective-permute-done((f32[128,1024]{0,1:T(8,128)S(1)}, f32[128,1024]{0,1:T(8,128)S(1)}, u32[]{:S(2)}, u32[]{:S(2)}) %collective-permute-start.9) | collective-permute-done | bytes 524320 | tf_op jit(solution)/shard_map/ppermute | solution.py:24
  377.4 6.7 fusion.54
  386.0 13.8 %collective-permute-done.3 = f32[128,1024]{1,0:T(8,128)S(1)} collective-permute-done((f32[128,1024]{1,0:T(8,128)S(1)}, f32[128,1024]{1,0:T(8,128)S(1)}, u32[]{:S(2)}, u32[]{:S(2)}) %collective-permute-start.3) | collective-permute-done | bytes 524320 | tf_op jit(solution)/shard_map/ppermute | solution.py:24
  406.3 67.2 %while.77 = (s32[]{:T(128)}, f32[1024]{0:T(1024)S(1)}, s32[8]{0:T(128)S(1)}, f32[2,1024,1024]{2,1,0:T(8,128)}, f32[8,1024]{1,0:T(8,128)S(1)}, /*index=5*/s32[]{:T(128)}, s32[]{:T(128)}, s32[]{:T(128)}) while((s32[]{:T(128)}, f32[1024]{0:T(1024)S(1)}, s32[8]{0:T(128)S(1)}, f32[2,1024,1024]{2,1,0:T(8,128)}, f32[8,1024]{1,0:T(8,128)S(1)}, ...), condition=%wide.region_1.2_spmd, body=%wide.region_0.1_spmd.sunk | while | flops 12583941 | bytes 4223115 | solution.py:94
  425.6 6.1 fusion.108
  434.2 5.8 fusion.108
  442.6 5.8 fusion.108
  477.9 12.0 %all-gather = f32[8,1,128]{2,1,0:T(1,128)S(1)} all-gather(f32[1,1,128]{2,1,0:T(1,128)S(1)} %bitcast.296), channel_id=1, replica_groups=mesh['tm'=16,'rows'=8] {'rows'}, dimensions={0}, use_global_device_ids=true | all-gather | bytes 4608 | tf_op jit(solution)/shard_map/all_gather | solution.py:43
  496.2 10.9 %all-gather.1 = f32[8,1,128]{2,1,0:T(1,128)S(1)} all-gather(f32[1,1,128]{2,1,0:T(1,128)S(1)} %bitcast.297), channel_id=1, replica_groups=mesh['tm'=16,'rows'=8] {'rows'}, dimensions={0}, use_global_device_ids=true | all-gather | bytes 4608 | tf_op jit(solution)/shard_map/all_gather | solution.py:43
  510.6 6.7 fusion.57
  520.7 8.4 all-gather.2
  538.5 10.9 %all-gather.3 = f32[8,1,128]{2,1,0:T(1,128)S(1)} all-gather(f32[1,1,128]{2,1,0:T(1,128)S(1)} %bitcast.293), channel_id=1, replica_groups=mesh['tm'=16,'rows'=8] {'rows'}, dimensions={0}, use_global_device_ids=true | all-gather | bytes 4608 | tf_op jit(solution)/shard_map/all_gather | solution.py:29
  554.2 9.0 all-gather.4
  569.4 10.9 %all-gather.5 = f32[8,1,128]{2,1,0:T(1,128)S(1)} all-gather(f32[1,1,128]{2,1,0:T(1,128)S(1)} %bitcast.288), channel_id=1, replica_groups=mesh['tm'=16,'rows'=8] {'rows'}, dimensions={0}, use_global_device_ids=true | all-gather | bytes 4608 | tf_op jit(solution)/shard_map/all_gather | solution.py:29
  580.3 67.2 %while.79 = (s32[]{:T(128)}, f32[1024]{0:T(1024)S(1)}, f32[8,1024]{1,0:T(8,128)S(1)}, s32[8]{0:T(128)S(1)}, f32[2,1024,1024]{2,1,0:T(8,128)}, /*index=5*/f32[8,1024]{1,0:T(8,128)S(1)}, s32[]{:T(128)}, s32[]{:T(128)}, s32[]{:T(128)}) while((s32[]{:T(128)}, f32[1024]{0:T(1024)S(1)}, f32[8,1024]{1,0:T(8,128)S(1)}, s32[8]{0:T(128)S(1)}, ...), condition=%wide.region_5.6_spmd, body=%wide.region_4.5_spmd.sunk | while | flops 12583941 | bytes 4231319 | solution.py:117
  582.7 5.8 fusion.114
  591.2 5.8 fusion.114
  653.1 76.8 %while.82 = (s32[]{:T(128)}, f32[1024]{0:T(1024)S(1)}, f32[8,1024]{1,0:T(8,128)S(1)}, f32[8]{0:T(128)S(1)}, s32[8]{0:T(128)S(1)}, /*index=5*/f32[2,1024,1024]{2,...) while((s32[]{:T(128)}, f32[1024]{0:T(1024)S(1)}, ...), condition=%wide.region_7.8_spmd.clone, body=%wide.region_6.7_spmd.clone.sunk | while | flops 12587015 | bytes 4243657 | solution.py:130
  655.7 5.8 fusion.123
  665.3 5.8 fusion.123
  674.9 5.8 fusion.123
  684.5 5.8 fusion.123
  694.1 5.8 fusion.123
  703.7 5.8 fusion.123
  713.3 5.8 fusion.123
  722.9 5.8 fusion.123
  736.4 8.9 all-gather.6
  752.4 11.0 %all-gather.7 = f32[8,1,128]{2,1,0:T(1,128)S(1)} all-gather(f32[1,1,128]{2,1,0:T(1,128)S(1)} %bitcast.299), channel_id=1, replica_groups=mesh['tm'=16,'rows'=8] {'rows'}, dimensions={0}, use_global_device_ids=true | all-gather | bytes 4608 | tf_op jit(solution)/shard_map/all_gather | solution.py:43
  771.2 8.1 all-gather.8
  784.1 10.9 %all-gather.9 = f32[8,1,128]{2,1,0:T(1,128)S(1)} all-gather(f32[1,1,128]{2,1,0:T(1,128)S(1)} %bitcast.295), channel_id=1, replica_groups=mesh['tm'=16,'rows'=8] {'rows'}, dimensions={0}, use_global_device_ids=true | all-gather | bytes 4608 | tf_op jit(solution)/shard_map/all_gather | solution.py:29
  799.9 9.0 all-gather.10
  815.8 10.9 %all-gather.11 = f32[8,1,128]{2,1,0:T(1,128)S(1)} all-gather(f32[1,1,128]{2,1,0:T(1,128)S(1)} %bitcast.292), channel_id=1, replica_groups=mesh['tm'=16,'rows'=8] {'rows'}, dimensions={0}, use_global_device_ids=true | all-gather | bytes 4608 | tf_op jit(solution)/shard_map/all_gather | solution.py:29
  826.7 74.7 %while.81 = (s32[]{:T(128)}, f32[1024]{0:T(1024)S(1)}, f32[8,1024]{1,0:T(8,128)S(1)}, f32[8,1024]{1,0:T(8,128)S(1)}, f32[8]{0:T(128)S(1)}, /*index=5*/s32[8]{0:T...) while((s32[]{:T(128)}, f32[1024]{0:T(1024)S(1)}, ...), condition=%wide.region_11.12_spmd, body=%wide.region_10.11_spmd.sunk | while | flops 12585990 | bytes 4251851 | solution.py:133
  829.0 5.8 fusion.120
  838.3 5.8 fusion.120
  847.7 5.8 fusion.120
  857.0 5.8 fusion.120
  866.3 5.8 fusion.120
  875.7 5.8 fusion.120
  (289 shorter events, 234.8 us)
Async XLA Ops:
  7.2 393.5 %copy-start = (f32[8,1024]{1,0:T(8,128)S(1)}, f32[8,1024]{1,0:T(8,128)}, u32[]{:S(2)}) copy-start(f32[8,1024]{1,0:T(8,128)} %param.20) | copy-start | bytes 98308
  7.2 106.3 %all-gather.20.cloned.1.call-start = ((), (), s32[]{:S(2)}) async-start(), calls=%async_computation.1 | async-start | bytes 4227072 | tf_op jit(solution)/shard_map/all_gather | solution.py:73
  7.9 220.3 %all-gather.26.cloned.1.call-start = ((), (), s32[]{:S(2)}) async-start(), calls=%async_computation.4 | async-start | bytes 4227072 | tf_op jit(solution)/shard_map/all_gather | solution.py:76
  8.7 243.2 %all-gather.28.cloned.1.call-start = ((), (), s32[]{:S(2)}) async-start(), calls=%async_computation.5 | async-start | bytes 4227072 | tf_op jit(solution)/shard_map/all_gather | solution.py:75
  12.7 60.1 %all-to-all-start = ((f32[128,8,1024]{2,1,0:T(8,128)}), f32[128,8,1024]{2,1,0:T(8,128)}, u32[]{:S(2)}, u32[]{:S(2)}) async-start(f32[128,8,1024]{2,1,0:T(8,128)} %stack.13), calls=%async_computation | async-start | bytes 8388608 | tf_op jit(solution)/shard_map/all_to_all | solution.py:12
  23.6 353.7 %all-gather.22.cloned.1.call-start = ((), (), s32[]{:S(2)}) async-start(), calls=%async_computation.2 | async-start | bytes 4718592 | tf_op jit(solution)/shard_map/all_gather | solution.py:42
  113.5 8.4 copy-start.6
  210.6 16.7 %collective-permute-start.1 = (f32[128,1024]{0,1:T(8,128)S(1)}, f32[128,1024]{0,1:T(8,128)S(1)}, u32[]{:S(2)}, u32[]{:S(2)}) collective-permute-start(f32[128,1024]{0,1:T(8,128)S(1)} %broadcast_multiply_fusion), channel_id=1, source_target_pairs={{0,8},{8,16},{16,24},{24,32},{32,40},{40,48},{48,56},{56,64},{64,7... | collective-permute-start | bytes 1572872 | tf_op jit(solution)/shard_map/ppermute | solution.py:24
  227.3 0.8 copy-start.4
  228.1 282.4 %all-gather.30.cloned.1.call-start = ((), (), s32[]{:S(2)}) async-start(), calls=%async_computation.6 | async-start | bytes 4718592 | tf_op jit(solution)/shard_map/all_gather | solution.py:42
  359.1 41.6 %copy-start.5 = (f32[1024]{0:T(1024)S(1)}, f32[1024]{0:T(1024)}, u32[]{:S(2)}) copy-start(f32[1024]{0:T(1024)} %param.22) | copy-start | bytes 12292
  359.1 17.2 %collective-permute-start.9 = (f32[128,1024]{0,1:T(8,128)S(1)}, f32[128,1024]{0,1:T(8,128)S(1)}, u32[]{:S(2)}, u32[]{:S(2)}) collective-permute-start(f32[128,1024]{0,1:T(8,128)S(1)} %get-tuple-element.477), channel_id=1, source_target_pairs={{8,0},{16,8},{24,16},{32,24},{40,32},{48,40},{56,48},{64,56},{72,6... | collective-permute-start | bytes 1572872 | tf_op jit(solution)/shard_map/ppermute | solution.py:24
  376.3 0.8 copy-start.2
  377.1 152.0 %all-gather.24.cloned.1.call-start = ((), (), s32[]{:S(2)}) async-start(), calls=%async_computation.3 | async-start | bytes 4718592 | tf_op jit(solution)/shard_map/all_gather | solution.py:42
  384.0 15.7 %collective-permute-start.3 = (f32[128,1024]{1,0:T(8,128)S(1)}, f32[128,1024]{1,0:T(8,128)S(1)}, u32[]{:S(2)}, u32[]{:S(2)}) collective-permute-start(f32[128,1024]{1,0:T(8,128)S(1)} %fusion.54), channel_id=1, source_target_pairs={{0,16},{8,24},{16,32},{24,40},{32,48},{40,56},{48,64},{56,72},{64,... | collective-permute-start | bytes 1572872 | tf_op jit(solution)/shard_map/ppermute | solution.py:24
  399.7 0.8 copy-start.3
  400.6 366.0 %all-gather.32.cloned.1.call-start = ((), (), s32[]{:S(2)}) async-start(), calls=%async_computation.7 | async-start | bytes 4718592 | tf_op jit(solution)/shard_map/all_gather | solution.py:42
  473.6 4.3 collective-permute-start
  490.3 5.8 collective-permute-start.2
  507.5 13.2 %collective-permute-start.4 = (f32[128]{0:T(128)S(1)}, f32[128]{0:T(128)S(1)}, u32[]{:S(2)}, u32[]{:S(2)}) collective-permute-start(f32[128]{0:T(128)S(1)} %fusion.41), channel_id=1, source_target_pairs={{0,32},{8,40},{16,48},{24,56},{32,64},{40,72},{48,80},{56,88},{64,... | collective-permute-start | bytes 1544 | tf_op jit(solution)/shard_map/ppermute | solution.py:24
  517.3 50.8 %collective-permute-start.11 = (f32[128,1024]{1,0:T(8,128)S(1)}, f32[128,1024]{1,0:T(8,128)S(1)}, u32[]{:S(2)}, u32[]{:S(2)}) collective-permute-start(f32[128,1024]{1,0:T(8,128)S(1)} %fusion.57), channel_id=1, source_target_pairs={{16,0},{24,8},{32,16},{40,24},{48,32},{56,40},{64,48},{72,56},{80,... | collective-permute-start | bytes 1572872 | tf_op jit(solution)/shard_map/ppermute | solution.py:24
  534.1 4.4 collective-permute-start.5
  549.9 4.4 collective-permute-start.6
  563.7 5.7 collective-permute-start.7
  568.1 0.8 copy-start.1
  730.0 6.4 collective-permute-start.8
  745.7 6.7 collective-permute-start.10
  763.8 7.4 collective-permute-start.12
  779.7 4.4 collective-permute-start.13
  795.5 4.4 collective-permute-start.14
  809.3 6.5 collective-permute-start.15
Sparse Core Ops, SparseCore 0:
  11.2 102.2 all-gather.19
  116.6 64.1 all-gather.25
  184.0 67.8 all-gather.27
  253.4 36.1 all-gather.21
  377.2 36.7 all-gather.29
  415.6 32.3 all-gather.23
  569.1 30.8 all-gather.31
